TPU v7x, 512 devices: a whole 4x4x16 slice. The times are simulated.
512 devices in a mesh: row: 16 (over z_lo, y), col: 32 (over z_hi, x, core).
Axes of the slice: x: 4, y: 4, z: 16 (z_hi: 4, z_lo: 4; z = z_hi * 4 + z_lo), core: 2. Of those that a mesh axis runs over, the one named last changes fastest.
Arguments:
- ancestor: float32 [20480, 20480], P('row', 'col'), as said below
- factor_rows: float32 [2, 256, 20480], P(None, 'row', 'col'), may hold values from -6 to 6
- block_lists: int32 [2, 8], replicated, may hold values from 0 to 15, as said below
Outputs:
- inverse_panel: float32 [2, 20480, 256], P(None, ('row', 'col'))
- inverse_rows: float32 [2, 256, 20480], P(None, 'col', 'row')
Inputs may be any that keep to these rules, and one draw needn't show every extreme that they name: `block_lists`: each row lists 8 distinct blocks in increasing order; the first block 0 and the last block 15 are in every row. ancestor is symmetric: ancestor[i, j] = ancestor[j, i].
All inputs are finite; a program needn't handle non-finite values.
Results may differ from a plain program's by a relative error of at most 0.000071.
Values sent between devices are 32-bit elements; how exact they have to be, the bound alone decides.
A program may use at most 64 MiB of HBM per device.

v0:
```python
import jax
import jax.numpy as jnp
from jax import lax
from jax.sharding import PartitionSpec as P

BS = 1280


def listed_mask(block_lists, blocks):
    return jnp.any(block_lists[:, :, None] == blocks[None, None, :], axis=1).astype(jnp.float32)


def per_device(ancestor, factor_rows, block_lists):
    local_rows = ancestor.shape[0]
    local_cols = ancestor.shape[1]
    col_count = lax.axis_size("col")
    row_place = lax.axis_index("row")
    col_place = lax.axis_index("col")
    col_blocks = (col_place * local_cols + lax.iota(jnp.int32, local_cols)) // BS
    masked = factor_rows * listed_mask(block_lists, col_blocks)[:, None, :]
    gathered = lax.all_gather(masked, "row", axis=1, tiled=True)
    rows_out = local_rows // col_count
    summed = lax.psum_scatter(
        -jnp.einsum(
            "ic,swc->isw",
            ancestor,
            gathered,
            precision=lax.Precision.HIGHEST,
            preferred_element_type=jnp.float32,
        ),
        "col",
        scatter_dimension=0,
        tiled=True,
    )
    first_row = (row_place * col_count + col_place) * rows_out
    row_mask = listed_mask(block_lists, (first_row + lax.iota(jnp.int32, rows_out)) // BS)
    inverse_panel = jnp.transpose(summed, (1, 0, 2)) * row_mask[:, :, None]
    arrived = lax.all_to_all(inverse_panel, "col", split_axis=2, concat_axis=1, tiled=True)
    inverse_rows = jnp.transpose(arrived, (0, 2, 1))
    return (inverse_panel, inverse_rows)


def solution(mesh):
    in_specs = (P("row", "col"), P(None, "row", "col"), P())
    out_specs = (P(None, ("row", "col"), None), P(None, "col", "row"))
    return jax.shard_map(
        per_device, mesh=mesh, in_specs=in_specs, out_specs=out_specs, check_vma=False
    )
```

profile of v0, /device:TPU:1, one launch (start us, length us, event | category | flops | bytes accessed | tf_op | source)
XLA Modules:
  0.0 525.2 jit_solution(5785872457603567026)
XLA Ops:
  7.2 0.0 copy-start
  7.2 0.0 all-gather.2.cloned.1.call-start
  7.2 0.9 compare_reduce_fusion
  8.2 1.5 broadcast_multiply_fusion
  9.7 0.0 all-gather.2.cloned.1.call-update
  9.7 0.0 all-reduce.3.cloned.1.call-start
  9.8 81.8 %all-gather.2.cloned.1.call-done = f32[2,256,640]{2,1,0:T(8,128)} async-done(((f32[2,16,640]{2,1,0:T(8,128)}), f32[2,256,640]{2,1,0:T(8,128)}) %all-gather.2.cloned.1.call-update) | async-done | bytes 1310736 | tf_op jit(solution)/shard_map/all_gather | solution.py:21
  91.6 0.0 copy-done
  91.6 9.2 %fusion.5 = f32[1280,2,256]{0,2,1:T(8,128)} fusion(f32[2,256,640]{2,1,0:T(8,128)} %all-gather.2.cloned.1.call-done, f32[1280,640]{1,0:T(8,128)S(1)} %copy-done), kind=kOutput, calls=%fused_computation.3 | convolution fusion | flops 5033820160 | bytes 7208960 | tf_op jit(solution)/shard_map/ic,swc->isw/dot_general | solution.py:24
  100.9 5.2 copy.11
  106.0 0.0 copy-start.1
  106.0 0.0 all-reduce.3.cloned.1.call-update
  106.1 0.6 copy-done.1
  106.7 0.1 compare_reduce_fusion.1
  106.8 0.1 copy.12
  106.9 1.3 dynamic-slice
  108.8 370.7 %all-reduce.3.cloned.1.call-done = f32[1280,2,256]{2,1,0:T(2,128)} async-done(((f32[1280,2,256]{2,1,0:T(2,128)}), f32[1280,2,256]{2,1,0:T(2,128)}) %all-reduce.3.cloned.1.call-update) | async-done | bytes 2621456
  479.5 1.6 fusion.8
  481.2 1.0 copy.13
  482.2 1.1 reshape.37
  483.3 14.3 %all-to-all-start = ((f32[32,1,640]{2,1,0:T(1,128)}), f32[32,1,640]{2,1,0:T(1,128)S(1)}, u32[]{:S(2)}, u32[]{:S(2)}) async-start(f32[32,1,640]{2,1,0:T(1,128)} %reshape.37), calls=%async_computation | async-start | bytes 163840 | tf_op jit(solution)/shard_map/all_to_all | solution.py:38
  497.6 1.5 copy.15
  499.1 13.2 %all-to-all-done = f32[32,1,640]{2,1,0:T(1,128)S(1)} async-done(((f32[32,1,640]{2,1,0:T(1,128)}), f32[32,1,640]{2,1,0:T(1,128)S(1)}, u32[]{:S(2)}, u32[]{:S(2)}) %all-to-all-start) | async-done | bytes 81952 | tf_op jit(solution)/shard_map/all_to_all | solution.py:38
  512.4 0.6 broadcast.51
  513.0 1.5 reduce
  514.5 1.3 reshape.38
  515.8 0.8 copy.14
  516.6 1.7 all_to_all.16
  (4 shorter events, 0.0 us)
Async XLA Ops:
  7.2 84.5 %copy-start = (f32[1280,640]{1,0:T(8,128)S(1)}, f32[1280,640]{1,0:T(8,128)}, u32[]{:S(2)}) copy-start(f32[1280,640]{1,0:T(8,128)} %param.3) | copy-start | bytes 9830404
  7.2 84.5 %all-gather.2.cloned.1.call-start = ((), (), s32[]{:S(2)}) async-start(), calls=%async_computation.1 | async-start | bytes 1392640 | tf_op jit(solution)/shard_map/all_gather | solution.py:21
  9.7 469.8 %all-reduce.3.cloned.1.call-start = ((), (), s32[]{:S(2)}) async-start(), calls=%async_computation.2 | async-start | bytes 5242880
  106.0 0.7 copy-start.1
  483.3 29.1 %all-to-all-start = ((f32[32,1,640]{2,1,0:T(1,128)}), f32[32,1,640]{2,1,0:T(1,128)S(1)}, u32[]{:S(2)}, u32[]{:S(2)}) async-start(f32[32,1,640]{2,1,0:T(1,128)} %reshape.37), calls=%async_computation | async-start | bytes 163840 | tf_op jit(solution)/shard_map/all_to_all | solution.py:38
Sparse Core Ops, SparseCore 0:
  10.6 80.9 all-gather.1
  106.2 373.3 all-reduce.2
where the time goes:
time: 526 us; the launch traced here: 525 us
  waiting for transfers between devices  466 us (89%)
  local copies, waits for them, and re-layouts  15.2 us (3%)
  between operations  14.8 us (3%)
  starting transfers between devices  14.4 us (3%)
  matrix products  9.24 us (2%)
  other arithmetic  5.73 us (1%)
    unnamed x3, waiting for transfers between devices  371 us
    all_gather x1, waiting for transfers between devices, per_device(): gathered = lax.all_gather(masked, 'row', axis=1, tiled=True)  81.8 us
    all_to_all x1, starting transfers between devices, per_device(): lax.all_to_all(inverse_panel, 'col', split_axis=2, concat_axis=1, tiled=T...  14.3 us
    all_to_all x1, waiting for transfers between devices, per_device(): lax.all_to_all(inverse_panel, 'col', split_axis=2, concat_axis=1, tiled=T...  13.2 us
  transfers between devices with their start and end apart: 3, of which 3 were waited for; matrix products, arithmetic and copies ran while one was open for 1% of the time, Pallas kernels for 0%

commit v1 on v0

--- a/solution.py
+++ b/solution.py
@@ -18,7 +18,8 @@
     col_place = lax.axis_index("col")
     col_blocks = (col_place * local_cols + lax.iota(jnp.int32, local_cols)) // BS
     masked = factor_rows * listed_mask(block_lists, col_blocks)[:, None, :]
-    gathered = lax.all_gather(masked, "row", axis=1, tiled=True)
+    sent = jnp.stack([masked] * lax.axis_size("row"))
+    gathered = jnp.concatenate(lax.all_to_all(sent, "row", 0, 0), axis=1)
     rows_out = local_rows // col_count
     summed = lax.psum_scatter(
         -jnp.einsum(

time: 526 us -> 475 us (0.903)
  waiting for transfers between devices: 466 us -> 376 us
  blocking collectives: 0 us -> 40.5 us
    all_gather x1 -> x0, waiting for transfers between devices: 81.8 us -> none  [per_device(): gathered = lax.all_gather(masked, 'row', axis=1, tiled=True)]
    all_to_all x0 -> x1, blocking collectives: none -> 40.5 us  [per_device(): gathered = jnp.concatenate(lax.all_to_all(sent, 'row', 0, 0), axis=1)]
    unnamed x3 -> x2, waiting for transfers between devices: 371 us -> 363 us
  transfers between devices with their start and end apart: 3 -> 2, of which waited for: 3 -> 2; matrix products, arithmetic and copies ran while one was open for 1% -> 1% of each run, Pallas kernels for 0% -> 0%
where the time goes in v1:
time: 475 us; the launch traced here: 474 us
  waiting for transfers between devices  376 us (79%)
  blocking collectives  40.5 us (9%)
  local copies, waits for them, and re-layouts  15.4 us (3%)
  between operations  14.8 us (3%)
  starting transfers between devices  14.3 us (3%)
  matrix products  7.96 us (2%)
  other arithmetic  5.1 us (1%)
    unnamed x2, waiting for transfers between devices  363 us
    all_to_all x1, blocking collectives, per_device(): gathered = jnp.concatenate(lax.all_to_all(sent, 'row', 0, 0), axis=1)  40.5 us
    all_to_all x1, starting transfers between devices, per_device(): lax.all_to_all(inverse_panel, 'col', split_axis=2, concat_axis=1, tiled=T...  14.3 us
    all_to_all x1, waiting for transfers between devices, per_device(): lax.all_to_all(inverse_panel, 'col', split_axis=2, concat_axis=1, tiled=T...  13.2 us
  transfers between devices with their start and end apart: 2, of which 2 were waited for; matrix products, arithmetic and copies ran while one was open for 1% of the time, Pallas kernels for 0%

profile of v1, /device:TPU:1, one launch (start us, length us, event | category | flops | bytes accessed | tf_op | source)
XLA Modules:
  0.0 474.1 jit_solution(17659881285091021186)
XLA Ops:
  7.2 0.0 copy-start
  7.2 0.0 all-reduce.3.cloned.1.call-start
  7.2 0.9 compare_reduce_fusion
  8.2 0.9 broadcast_multiply_fusion
  9.1 0.1 stack.2
  9.2 40.5 %all_to_all.23 = f32[16,2,16,640]{3,2,1,0:T(8,128)S(1)} all-to-all(f32[16,2,16,640]{3,2,1,0:T(8,128)S(1)} %stack.2), channel_id=1, replica_groups=mesh['row'=16,'col'=32] {'row'}, dimensions={0} | all-to-all | bytes 2621440 | tf_op jit(solution)/shard_map/all_to_all | solution.py:22
  49.7 0.1 copy.12
  49.8 0.0 copy-done
  49.9 8.0 %fusion.5 = f32[1280,2,256]{0,2,1:T(8,128)} fusion(f32[2,256,640]{2,1,0:T(8,128)S(1)} %bitcast.27, f32[1280,640]{1,0:T(8,128)S(1)} %copy-done), kind=kOutput, calls=%fused_computation.3 | convolution fusion | flops 5033820160 | bytes 7208960 | tf_op jit(solution)/shard_map/ic,swc->isw/dot_general | solution.py:25
  57.8 5.1 %copy.13 = f32[1280,2,256]{2,1,0:T(2,128)} copy(f32[1280,2,256]{0,2,1:T(8,128)} %fusion.5) | data formatting | bytes 5242880 | tf_op jit(solution)/shard_map/neg | solution.py:25
  63.0 0.0 copy-start.1
  63.0 0.0 all-reduce.3.cloned.1.call-update
  63.0 0.6 copy-done.1
  63.6 0.1 compare_reduce_fusion.1
  63.7 0.1 copy.14
  63.8 1.3 dynamic-slice
  65.7 362.7 %all-reduce.3.cloned.1.call-done = f32[1280,2,256]{2,1,0:T(2,128)} async-done(((f32[1280,2,256]{2,1,0:T(2,128)}), f32[1280,2,256]{2,1,0:T(2,128)}) %all-reduce.3.cloned.1.call-update) | async-done | bytes 2621456
  428.5 1.6 fusion.8
  430.1 1.0 copy.15
  431.1 1.1 reshape.47
  432.2 14.3 %all-to-all-start.1 = ((f32[32,1,640]{2,1,0:T(1,128)}), f32[32,1,640]{2,1,0:T(1,128)S(1)}, u32[]{:S(2)}, u32[]{:S(2)}) async-start(f32[32,1,640]{2,1,0:T(1,128)} %reshape.47), calls=%async_computation.1 | async-start | bytes 163840 | tf_op jit(solution)/shard_map/all_to_all | solution.py:39
  446.5 1.5 copy.17
  448.1 13.2 %all-to-all-done.1 = f32[32,1,640]{2,1,0:T(1,128)S(1)} async-done(((f32[32,1,640]{2,1,0:T(1,128)}), f32[32,1,640]{2,1,0:T(1,128)S(1)}, u32[]{:S(2)}, u32[]{:S(2)}) %all-to-all-start.1) | async-done | bytes 81952 | tf_op jit(solution)/shard_map/all_to_all | solution.py:39
  461.3 0.6 broadcast.53
  461.9 1.5 reduce
  463.4 1.3 reshape.48
  464.7 0.8 copy.16
  465.5 1.7 all_to_all.20
  (4 shorter events, 0.0 us)
Async XLA Ops:
  7.2 42.7 %copy-start = (f32[1280,640]{1,0:T(8,128)S(1)}, f32[1280,640]{1,0:T(8,128)}, u32[]{:S(2)}) copy-start(f32[1280,640]{1,0:T(8,128)} %param.3) | copy-start | bytes 9830404
  7.2 421.3 %all-reduce.3.cloned.1.call-start = ((), (), s32[]{:S(2)}) async-start(), calls=%async_computation.2 | async-start | bytes 5242880
  63.0 0.7 copy-start.1
  432.2 29.1 %all-to-all-start.1 = ((f32[32,1,640]{2,1,0:T(1,128)}), f32[32,1,640]{2,1,0:T(1,128)S(1)}, u32[]{:S(2)}, u32[]{:S(2)}) async-start(f32[32,1,640]{2,1,0:T(1,128)} %reshape.47), calls=%async_computation.1 | async-start | bytes 163840 | tf_op jit(solution)/shard_map/all_to_all | solution.py:39
Sparse Core Ops, SparseCore 0:
  63.1 365.3 all-reduce.2
